TPU v7x, 512 devices: a whole 4x8x8 slice. The times are simulated.
512 devices in a mesh: ctx: 64 (over x, z, core), kvh: 8 (over y).
Axes of the slice: x: 4, y: 8, z: 8, core: 2. Of those that a mesh axis runs over, the one named last changes fastest.
Arguments:
- queries: bfloat16 [32768, 8192], P('ctx', 'kvh')
- key_vector_rows: bfloat16 [32768, 1024], P('ctx', 'kvh')
- value_vector_rows: bfloat16 [32768, 1024], P('ctx', 'kvh'), may hold values from -6 to 6
- block_picks: int32 [256, 8], P('ctx'), may hold values from 0 to 255, as said below
Outputs:
- attended: bfloat16 [32768, 8192], P(('ctx', 'kvh'))
Inputs may be any that keep to these rules, and one draw needn't show every extreme that they name: block_picks[b, 0] = b. The other entries of a row name 7 distinct blocks that lie on other indices of ctx (block c lies on index c // 4). Over the 4 rows of one index of ctx, the entries naming blocks of any one other index are at most 2 and name at most 1 distinct blocks; both bounds are reached in every draw.
All inputs are finite; a program needn't handle non-finite values.
Results may differ from a plain program's by a relative error of at most 0.0047.
Values may be sent and summed in bfloat16 or wider, within the bound.
No kernel may reach another device: no remote copies, remote signals or barrier semaphores. Data moves between devices by JAX's collectives and lax.ppermute only.
A program may use at most 64 MiB of HBM per device.

v0:
```python
import math

import jax
import jax.numpy as jnp
from jax import lax
from jax.experimental import pallas as pl
from jax.experimental.pallas import tpu as pltpu
from jax.sharding import PartitionSpec as P


HEAD_SIZE = 128
BLOCK_TOKENS = 128
PICKED_BLOCKS = 8
SIZE_X, SIZE_Z, CORES = 4, 8, 2
OFFSETS = (0, 1, -1, -2, 2, 3, -3, -4)
BATCHES = ((0, 1), (2, 3), (4, 5, 6, 7))


def pack_kernel(k_ref, v_ref, out_ref, sem):
    for b in range(out_ref.shape[0]):
        rows = pl.ds(b * BLOCK_TOKENS, BLOCK_TOKENS)
        for part, ref in enumerate((k_ref, v_ref)):
            target = out_ref.at[b, pl.ds(part * BLOCK_TOKENS, BLOCK_TOKENS)]
            pltpu.make_async_copy(ref.at[rows], target, sem).start()
    pltpu.make_async_copy(out_ref, out_ref, sem).wait()


def pack(keys, values):
    rows, width = keys.shape
    return pl.pallas_call(
        pack_kernel,
        out_shape=jax.ShapeDtypeStruct((rows // BLOCK_TOKENS, 2 * BLOCK_TOKENS, width), keys.dtype),
        in_specs=[pl.BlockSpec(memory_space=pl.ANY)] * 2,
        out_specs=pl.BlockSpec(memory_space=pltpu.VMEM),
        scratch_shapes=[pltpu.SemaphoreType.DMA],
        compiler_params=pltpu.CompilerParams(vmem_limit_bytes=PACK_GRANT),
        cost_estimate=pl.CostEstimate(flops=0, bytes_accessed=8 * rows * width, transcendentals=0),
        name="pack",
    )(keys, values)


def pick_kernel(slots, sources, wanted, *refs):
    shards, out_ref = refs[:-1], refs[-1]

    @pl.loop(0, out_ref.shape[0])
    def _(d):
        for n, (slot, (which, first)) in enumerate(zip(slots, sources)):
            out_ref[d, n] = shards[which][first + wanted[d, slot]]


GRANT = 16 * 2**20
PACK_GRANT = 60 * 2**20
ATTEND_GRANT = 48 * 2**20


def pick_blocks(wanted, slots, sources, shards):
    group = SIZE_X * CORES
    shape = (group, len(slots), 2 * BLOCK_TOKENS, HEAD_SIZE)
    return pl.pallas_call(
        lambda *refs: pick_kernel(slots, sources, *refs),
        out_shape=jax.ShapeDtypeStruct(shape, shards[0].dtype),
        grid_spec=pltpu.PrefetchScalarGridSpec(
            num_scalar_prefetch=1,
            in_specs=[pl.BlockSpec(memory_space=pltpu.VMEM)] * len(shards),
            out_specs=pl.BlockSpec(memory_space=pltpu.VMEM),
        ),
        compiler_params=pltpu.CompilerParams(vmem_limit_bytes=GRANT),
        cost_estimate=pl.CostEstimate(flops=0, bytes_accessed=4 * math.prod(shape), transcendentals=0),
        name="pick_blocks",
    )(wanted, *shards)


def attend_kernel(batches, table, q_ref, k_ref, v_ref, *rest):
    fetched = rest[:batches]
    out_ref, q_buf, kv_buf, sem = rest[batches:]
    row = pl.program_id(0)
    heads = q_ref.shape[1] // HEAD_SIZE

    def fetch(r):
        side = lax.rem(r, 2)
        own = pl.ds(pl.multiple_of(r * BLOCK_TOKENS, BLOCK_TOKENS), BLOCK_TOKENS)
        for part, ref in enumerate((k_ref, v_ref)):
            target = kv_buf.at[side, 0, pl.ds(part * BLOCK_TOKENS, BLOCK_TOKENS)]
            pltpu.make_async_copy(ref.at[own], target, sem.at[side]).start()
        for j in range(1, PICKED_BLOCKS):
            for n, ref in enumerate(fetched):
                index = table[n, r * PICKED_BLOCKS + j]

                @pl.when(index >= 0)
                def _(ref=ref, index=index):
                    pltpu.make_async_copy(ref.at[index], kv_buf.at[side, j], sem.at[side]).start()

    @pl.when(row == 0)
    def _():
        fetch(0)

    for h in range(heads):
        q_buf[pl.ds(h * BLOCK_TOKENS, BLOCK_TOKENS), :] = q_ref[:, pl.ds(h * HEAD_SIZE, HEAD_SIZE)]
    side = lax.rem(row, 2)
    pltpu.make_async_copy(kv_buf.at[side], kv_buf.at[side], sem.at[side]).wait()

    @pl.when(row + 1 < pl.num_programs(0))
    def _():
        fetch(row + 1)

    span = PICKED_BLOCKS * BLOCK_TOKENS
    keys = kv_buf[side, :, pl.ds(0, BLOCK_TOKENS), :].reshape(span, HEAD_SIZE)
    values = kv_buf[side, :, pl.ds(BLOCK_TOKENS, BLOCK_TOKENS), :].reshape(span, HEAD_SIZE)
    factor = math.log2(math.e) / math.sqrt(HEAD_SIZE)
    PAIR = 2
    shape = (PAIR * BLOCK_TOKENS, BLOCK_TOKENS)
    causal = lax.broadcasted_iota(jnp.int32, shape, 1) <= lax.broadcasted_iota(jnp.int32, shape, 0) % BLOCK_TOKENS

    def score(h):
        return lax.dot_general(
            q_buf[pl.ds(h * BLOCK_TOKENS, PAIR * BLOCK_TOKENS), :],
            keys,
            (((1,), (1,)), ((), ())),
            preferred_element_type=jnp.float32,
        )

    following = score(0)
    for h in range(0, heads, PAIR):
        scores = following
        if h + PAIR < heads:
            following = score(h + PAIR)
        own = jnp.where(causal, scores[:, :BLOCK_TOKENS], -jnp.inf)
        scores = jnp.concatenate([own, scores[:, BLOCK_TOKENS:]], axis=1)
        row_max = jnp.max(scores, axis=1, keepdims=True)
        exponents = jnp.exp2((scores - row_max) * factor)
        totals = jnp.sum(exponents, axis=1, keepdims=True)
        blended = jnp.dot(exponents.astype(jnp.bfloat16), values, preferred_element_type=jnp.float32)
        result = (blended / totals).astype(out_ref.dtype)
        for n in range(PAIR):
            out_ref[:, pl.ds((h + n) * HEAD_SIZE, HEAD_SIZE)] = result[n * BLOCK_TOKENS : (n + 1) * BLOCK_TOKENS]


def attend(column, slot, queries, keys, values, fetched):
    rows, width = queries.shape
    blocks = rows // BLOCK_TOKENS
    table, first = [], 0
    for f in fetched:
        size = f.shape[1]
        inside = (slot >= first) & (slot < first + size)
        table.append(jnp.where(inside, column * size + slot - first, -1))
        first += size
    fetched = [f.reshape(-1, *f.shape[2:]) for f in fetched]
    anywhere = pl.BlockSpec(memory_space=pl.ANY)
    return pl.pallas_call(
        lambda *refs: attend_kernel(len(fetched), *refs),
        out_shape=jax.ShapeDtypeStruct((rows, width), jnp.bfloat16),
        grid_spec=pltpu.PrefetchScalarGridSpec(
            num_scalar_prefetch=1,
            grid=(blocks,),
            in_specs=[pl.BlockSpec((BLOCK_TOKENS, width), lambda i, s: (i, 0))] + [anywhere] * (2 + len(fetched)),
            out_specs=pl.BlockSpec((BLOCK_TOKENS, width), lambda i, s: (i, 0)),
            scratch_shapes=[
                pltpu.VMEM((width // HEAD_SIZE * BLOCK_TOKENS, HEAD_SIZE), jnp.bfloat16),
                pltpu.VMEM((2, PICKED_BLOCKS, 2 * BLOCK_TOKENS, HEAD_SIZE), jnp.bfloat16),
                pltpu.SemaphoreType.DMA((2,)),
            ],
        ),
        compiler_params=pltpu.CompilerParams(vmem_limit_bytes=ATTEND_GRANT),
        name="attend",
    )(jnp.stack([t.reshape(-1) for t in table]), queries, keys, values, *fetched)


def flat(x, z, c):
    return (x % SIZE_X * SIZE_Z + z % SIZE_Z) * CORES + c


CHIPS = [(x, z, c) for x in range(SIZE_X) for z in range(SIZE_Z) for c in range(CORES)]
FIRST = [(flat(x, z, c), flat(x, z + 1 - 2 * ((z + c) % 2), c)) for x, z, c in CHIPS]
SECOND = [(flat(x, z, c), flat(x, z - 1 + 2 * ((z + c) % 2), c)) for x, z, c in CHIPS]
ROWS = [[flat(x, z, c) for x in range(SIZE_X) for c in range(CORES)] for z in range(SIZE_Z)]


def to_row(array):
    return lax.all_to_all(array, "ctx", split_axis=0, concat_axis=0, axis_index_groups=ROWS)


def attention(queries, key_vector_rows, value_vector_rows, block_picks):
    blocks = key_vector_rows.shape[0] // BLOCK_TOKENS
    group = SIZE_X * CORES
    my_z = lax.axis_index("ctx") // CORES % SIZE_Z
    owners, local_ids = block_picks // blocks, block_picks % blocks
    owner_x, owner_z, owner_core = owners // (SIZE_Z * CORES), owners // CORES % SIZE_Z, owners % CORES
    distance = owner_z - my_z
    distance = jnp.where((my_z + owner_core) % 2 == 0, distance, -distance) % SIZE_Z
    slot = jnp.zeros_like(distance)
    for s, d in enumerate(OFFSETS):
        slot = jnp.where(distance == d % SIZE_Z, s, slot)
    column = owner_x * CORES + owner_core
    places = column * SIZE_Z + slot
    far, far_ids = places[:, 1:].reshape(1, -1), local_ids[:, 1:].reshape(1, -1)
    hits = far == jnp.arange(group * SIZE_Z, dtype=jnp.int32)[:, None]
    requests = jnp.max(jnp.where(hits, far_ids, 0), axis=1).reshape(group, SIZE_Z)
    wanted = to_row(requests)

    shard = pack(key_vector_rows, value_vector_rows)
    other = lax.ppermute(shard, "ctx", FIRST)
    pairs = [jnp.concatenate([shard, other], axis=0)]
    for n in range(1, 4):
        pairs.append(lax.ppermute(pairs[-1], "ctx", SECOND if n % 2 else FIRST))

    origin = {s: (pairs[s // 2], s % 2 * blocks) for s in range(SIZE_Z)}
    fetched = []
    for slots in BATCHES:
        arrays, sources = [], []
        for s in slots:
            array, first = origin[s]
            which = next((i for i, a in enumerate(arrays) if a is array), None)
            if which is None:
                which = len(arrays)
                arrays.append(array)
            sources.append((which, first))
        outgoing = pick_blocks(wanted, slots, sources, arrays)
        fetched.append(to_row(outgoing))
    attended = attend(column, slot, queries, key_vector_rows, value_vector_rows, fetched)
    return lax.all_to_all(attended, "kvh", split_axis=0, concat_axis=1, tiled=True)


def solution(mesh):
    return jax.shard_map(
        attention,
        mesh=mesh,
        in_specs=(P("ctx", "kvh"), P("ctx", "kvh"), P("ctx", "kvh"), P("ctx", None)),
        out_specs=P(("ctx", "kvh"), None),
        check_vma=False,
    )
```

profile of v0, /device:TPU:1, one launch (start us, length us, event | category | flops | bytes accessed | tf_op | source)
XLA Modules:
  0.0 143.3 jit_solution(13874104822670321484)
XLA Ops:
  0.0 1.6 %pack.1 = bf16[4,256,128]{2,1,0:T(8,128)(2,1)} custom-call(bf16[512,128]{1,0:T(8,128)(2,1)} %refs_2_.1, bf16[512,128]{1,0:T(8,128)(2,1)} %refs_3_.1), custom_call_target="tpu_custom_call" | custom-call | bytes 524288 | tf_op jit(solution)/shard_map/pack/pallas_call | solution.py:30
  1.6 11.5 %collective-permute-start = (bf16[4,256,128]{2,1,0:T(8,128)(2,1)}, bf16[4,256,128]{2,1,0:T(8,128)(2,1)S(1)}, u32[]{:S(2)}, u32[]{:S(2)}) collective-permute-start(bf16[4,256,128]{2,1,0:T(8,128)(2,1)} %pack.1), channel_id=1, source_target_pairs={{0,16},{8,120},{16,0},{24,40},{32,48},{40,24},{48,32},{56,72},{64,... | collective-permute-start | bytes 786440 | tf_op jit(solution)/shard_map/ppermute | solution.py:201
  13.1 0.7 multiply_add_fusion
  13.8 0.1 slice.6
  13.9 0.1 eq.64
  14.1 0.1 broadcast_in_dim.31
  14.1 0.1 select_reduce_fusion
  14.2 0.7 all_to_all.30
  14.9 4.4 %all-to-all-start = ((s32[8,1,8]{2,1,0:T(1,128)}), s32[8,1,8]{2,1,0:T(1,128)S(1)}, u32[]{:S(2)}, u32[]{:S(2)}) async-start(s32[8,1,8]{2,1,0:T(1,128)} %bitcast), calls=%async_computation | async-start | bytes 8192 | tf_op jit(solution)/shard_map/all_to_all | solution.py:179
  19.3 1.0 pad_maximum_fusion.refs_1_
  20.3 3.6 %all-to-all-done = s32[8,1,8]{2,1,0:T(1,128)S(1)} async-done(((s32[8,1,8]{2,1,0:T(1,128)}), s32[8,1,8]{2,1,0:T(1,128)S(1)}, u32[]{:S(2)}, u32[]{:S(2)}) %all-to-all-start) | async-done | bytes 288 | tf_op jit(solution)/shard_map/all_to_all | solution.py:179
  23.9 1.7 %pick_blocks.3 = bf16[8,2,256,128]{3,2,1,0:T(8,128)(2,1)} custom-call(s32[8,8]{1,0:T(8,128)S(1)} %bitcast.12, bf16[8,256,128]{2,1,0:T(8,128)(2,1)S(1)} %pad_maximum_fusion.refs_1_), custom_call_target="tpu_custom_call" | custom-call | bytes 2097152 | tf_op jit(solution)/shard_map/pick_blocks/pallas_call | solution.py:59
  25.6 4.2 %all-to-all-start.1 = ((bf16[8,2,256,128]{3,2,1,0:T(8,128)(2,1)}), bf16[8,2,256,128]{3,2,1,0:T(8,128)(2,1)S(1)}, u32[]{:S(2)}, u32[]{:S(2)}) async-start(bf16[8,2,256,128]{3,2,1,0:T(8,128)(2,1)} %pick_blocks.3), calls=%async_computation.1 | async-start | bytes 2097152 | tf_op jit(solution)/shard_map/all_to_all | solution.py:179
  29.8 1.9 %collective-permute-start.1 = (bf16[8,256,128]{2,1,0:T(8,128)(2,1)S(1)}, bf16[8,256,128]{2,1,0:T(8,128)(2,1)S(1)}, u32[]{:S(2)}, u32[]{:S(2)}) collective-permute-start(bf16[8,256,128]{2,1,0:T(8,128)(2,1)S(1)} %pad_maximum_fusion.refs_1_), channel_id=1, source_target_pairs={{0,112},{8,24},{16,32},{24,8},{32,16},{40,56},{48,64},{56,40},{64,... | collective-permute-start | bytes 1572872 | tf_op jit(solution)/shard_map/ppermute | solution.py:204
  31.7 8.3 %collective-permute-done.1.refs_1_ = bf16[8,256,128]{2,1,0:T(8,128)(2,1)S(1)} collective-permute-done((bf16[8,256,128]{2,1,0:T(8,128)(2,1)S(1)}, bf16[8,256,128]{2,1,0:T(8,128)(2,1)S(1)}, u32[]{:S(2)}, u32[]{:S(2)}) %collective-permute-start.1) | collective-permute-done | bytes 524320 | tf_op jit(solution)/shard_map/ppermute | solution.py:204
  40.0 3.0 %collective-permute-start.2 = (bf16[8,256,128]{2,1,0:T(8,128)(2,1)S(1)}, bf16[8,256,128]{2,1,0:T(8,128)(2,1)S(1)}, u32[]{:S(2)}, u32[]{:S(2)}) collective-permute-start(bf16[8,256,128]{2,1,0:T(8,128)(2,1)S(1)} %collective-permute-done.1.refs_1_), channel_id=1, source_target_pairs={{0,16},{8,120},{16,0},{24,40},{32,48},{40,24},{48,32},{56,72},{64,... | collective-permute-start | bytes 1572872 | tf_op jit(solution)/shard_map/ppermute | solution.py:204
  43.0 1.7 %pick_blocks.4 = bf16[8,2,256,128]{3,2,1,0:T(8,128)(2,1)} custom-call(s32[8,8]{1,0:T(8,128)S(1)} %bitcast.13, bf16[8,256,128]{2,1,0:T(8,128)(2,1)S(1)} %collective-permute-done.1.refs_1_), custom_call_target="tpu_custom_call" | custom-call | bytes 2097152 | tf_op jit(solution)/shard_map/pick_blocks/pallas_call | solution.py:59
  44.7 0.1 all-to-all-done.1
  44.8 5.7 %all-to-all-start.2 = ((bf16[8,2,256,128]{3,2,1,0:T(8,128)(2,1)}), bf16[8,2,256,128]{3,2,1,0:T(8,128)(2,1)S(1)}, u32[]{:S(2)}, u32[]{:S(2)}) async-start(bf16[8,2,256,128]{3,2,1,0:T(8,128)(2,1)} %pick_blocks.4), calls=%async_computation.2 | async-start | bytes 2097152 | tf_op jit(solution)/shard_map/all_to_all | solution.py:179
  50.5 0.6 collective-permute-done.2.refs_1_
  51.1 3.0 %collective-permute-start.3 = (bf16[8,256,128]{2,1,0:T(8,128)(2,1)S(1)}, bf16[8,256,128]{2,1,0:T(8,128)(2,1)S(1)}, u32[]{:S(2)}, u32[]{:S(2)}) collective-permute-start(bf16[8,256,128]{2,1,0:T(8,128)(2,1)S(1)} %collective-permute-done.2.refs_1_), channel_id=1, source_target_pairs={{0,112},{8,24},{16,32},{24,8},{32,16},{40,56},{48,64},{56,40},{64,... | collective-permute-start | bytes 1572872 | tf_op jit(solution)/shard_map/ppermute | solution.py:204
  54.1 7.2 %collective-permute-done.3.refs_2_ = bf16[8,256,128]{2,1,0:T(8,128)(2,1)S(1)} collective-permute-done((bf16[8,256,128]{2,1,0:T(8,128)(2,1)S(1)}, bf16[8,256,128]{2,1,0:T(8,128)(2,1)S(1)}, u32[]{:S(2)}, u32[]{:S(2)}) %collective-permute-start.3) | collective-permute-done | bytes 524320 | tf_op jit(solution)/shard_map/ppermute | solution.py:204
  61.3 2.1 %pick_blocks.5 = bf16[8,4,256,128]{3,2,1,0:T(8,128)(2,1)} custom-call(s32[8,8]{1,0:T(8,128)S(1)} %bitcast.14, bf16[8,256,128]{2,1,0:T(8,128)(2,1)S(1)} %collective-permute-done.2.refs_1_, bf16[8,256,128]{2,1,0:T(8,128)(2,1)S(1)} %collective-permute-done.3.refs_2_), custom_call_target="tpu_custom_call" | custom-call | bytes 4194304 | tf_op jit(solution)/shard_map/pick_blocks/pallas_call | solution.py:59
  63.4 2.0 %all-to-all-done.2 = bf16[8,2,256,128]{3,2,1,0:T(8,128)(2,1)S(1)} async-done(((bf16[8,2,256,128]{3,2,1,0:T(8,128)(2,1)}), bf16[8,2,256,128]{3,2,1,0:T(8,128)(2,1)S(1)}, u32[]{:S(2)}, u32[]{:S(2)}) %all-to-all-start.2) | async-done | bytes 1048608 | tf_op jit(solution)/shard_map/all_to_all | solution.py:179
  65.4 7.0 %all-to-all-start.3 = ((bf16[8,4,256,128]{3,2,1,0:T(8,128)(2,1)}), bf16[8,4,256,128]{3,2,1,0:T(8,128)(2,1)}, u32[]{:S(2)}, u32[]{:S(2)}) async-start(bf16[8,4,256,128]{3,2,1,0:T(8,128)(2,1)} %pick_blocks.5), calls=%async_computation.3 | async-start | bytes 4194304 | tf_op jit(solution)/shard_map/all_to_all | solution.py:179
  72.5 0.1 stack_reshape.9
  72.6 0.1 stack_reshape.10
  72.7 0.1 stack_reshape.11
  72.8 26.0 %all-to-all-done.3 = bf16[8,4,256,128]{3,2,1,0:T(8,128)(2,1)} async-done(((bf16[8,4,256,128]{3,2,1,0:T(8,128)(2,1)}), bf16[8,4,256,128]{3,2,1,0:T(8,128)(2,1)}, u32[]{:S(2)}, u32[]{:S(2)}) %all-to-all-start.3) | async-done | bytes 2097184 | tf_op jit(solution)/shard_map/all_to_all | solution.py:179
  98.8 9.8 %attend.1 = bf16[512,1024]{1,0:T(8,128)(2,1)S(1)} custom-call(s32[3,32]{1,0:T(4,128)S(1)} %pad_add_fusion.refs_0_, bf16[512,1024]{1,0:T(8,128)(2,1)S(1)} %copy-done, bf16[512,128]{1,0:T(8,128)(2,1)S(1)} %copy-done.1, bf16[512,128]{1,0:T(8,128)(2,1)S(1)} %copy-done.2, bf16[16,256,128]{2,1,0:T(8,128)(2,1)S(1)} %bitcast.9, bf16[16,256,128]{2,1,0:T(8,128)(2,1)S(1)} %bitcast.10, ...), custom_call_target="tpu_custom_call" | custom-call | tf_op jit(solution)/shard_map/attend/pallas_call | solution.py:149
  108.6 33.6 %all_to_all.45 = bf16[8,64,1024]{2,1,0:T(8,128)(2,1)S(1)} all-to-all(bf16[8,64,1024]{2,1,0:T(8,128)(2,1)S(1)} %bitcast.11), channel_id=1, replica_groups=mesh['ctx'=64,'kvh'=8] {'kvh'}, dimensions={0} | all-to-all | bytes 2097152 | tf_op jit(solution)/shard_map/all_to_all | solution.py:220
  142.2 1.1 copy.10
  (10 shorter events, 0.1 us)
Async XLA Ops:
  1.6 17.8 %collective-permute-start = (bf16[4,256,128]{2,1,0:T(8,128)(2,1)}, bf16[4,256,128]{2,1,0:T(8,128)(2,1)S(1)}, u32[]{:S(2)}, u32[]{:S(2)}) collective-permute-start(bf16[4,256,128]{2,1,0:T(8,128)(2,1)} %pack.1), channel_id=1, source_target_pairs={{0,16},{8,120},{16,0},{24,40},{32,48},{40,24},{48,32},{56,72},{64,... | collective-permute-start | bytes 786440 | tf_op jit(solution)/shard_map/ppermute | solution.py:201
  14.9 9.0 %all-to-all-start = ((s32[8,1,8]{2,1,0:T(1,128)}), s32[8,1,8]{2,1,0:T(1,128)S(1)}, u32[]{:S(2)}, u32[]{:S(2)}) async-start(s32[8,1,8]{2,1,0:T(1,128)} %bitcast), calls=%async_computation | async-start | bytes 8192 | tf_op jit(solution)/shard_map/all_to_all | solution.py:179
  25.6 19.2 %all-to-all-start.1 = ((bf16[8,2,256,128]{3,2,1,0:T(8,128)(2,1)}), bf16[8,2,256,128]{3,2,1,0:T(8,128)(2,1)S(1)}, u32[]{:S(2)}, u32[]{:S(2)}) async-start(bf16[8,2,256,128]{3,2,1,0:T(8,128)(2,1)} %pick_blocks.3), calls=%async_computation.1 | async-start | bytes 2097152 | tf_op jit(solution)/shard_map/all_to_all | solution.py:179
  29.8 10.2 %collective-permute-start.1 = (bf16[8,256,128]{2,1,0:T(8,128)(2,1)S(1)}, bf16[8,256,128]{2,1,0:T(8,128)(2,1)S(1)}, u32[]{:S(2)}, u32[]{:S(2)}) collective-permute-start(bf16[8,256,128]{2,1,0:T(8,128)(2,1)S(1)} %pad_maximum_fusion.refs_1_), channel_id=1, source_target_pairs={{0,112},{8,24},{16,32},{24,8},{32,16},{40,56},{48,64},{56,40},{64,... | collective-permute-start | bytes 1572872 | tf_op jit(solution)/shard_map/ppermute | solution.py:204
  40.0 11.1 %collective-permute-start.2 = (bf16[8,256,128]{2,1,0:T(8,128)(2,1)S(1)}, bf16[8,256,128]{2,1,0:T(8,128)(2,1)S(1)}, u32[]{:S(2)}, u32[]{:S(2)}) collective-permute-start(bf16[8,256,128]{2,1,0:T(8,128)(2,1)S(1)} %collective-permute-done.1.refs_1_), channel_id=1, source_target_pairs={{0,16},{8,120},{16,0},{24,40},{32,48},{40,24},{48,32},{56,72},{64,... | collective-permute-start | bytes 1572872 | tf_op jit(solution)/shard_map/ppermute | solution.py:204
  44.8 20.7 %all-to-all-start.2 = ((bf16[8,2,256,128]{3,2,1,0:T(8,128)(2,1)}), bf16[8,2,256,128]{3,2,1,0:T(8,128)(2,1)S(1)}, u32[]{:S(2)}, u32[]{:S(2)}) async-start(bf16[8,2,256,128]{3,2,1,0:T(8,128)(2,1)} %pick_blocks.4), calls=%async_computation.2 | async-start | bytes 2097152 | tf_op jit(solution)/shard_map/all_to_all | solution.py:179
  51.1 10.2 %collective-permute-start.3 = (bf16[8,256,128]{2,1,0:T(8,128)(2,1)S(1)}, bf16[8,256,128]{2,1,0:T(8,128)(2,1)S(1)}, u32[]{:S(2)}, u32[]{:S(2)}) collective-permute-start(bf16[8,256,128]{2,1,0:T(8,128)(2,1)S(1)} %collective-permute-done.2.refs_1_), channel_id=1, source_target_pairs={{0,112},{8,24},{16,32},{24,8},{32,16},{40,56},{48,64},{56,40},{64,... | collective-permute-start | bytes 1572872 | tf_op jit(solution)/shard_map/ppermute | solution.py:204
  63.4 35.4 %copy-start = (bf16[512,1024]{1,0:T(8,128)(2,1)S(1)}, bf16[512,1024]{1,0:T(8,128)(2,1)}, u32[]{:S(2)}) copy-start(bf16[512,1024]{1,0:T(8,128)(2,1)} %refs_1_.1) | copy-start | bytes 3145732
  63.4 35.4 %copy-start.1 = (bf16[512,128]{1,0:T(8,128)(2,1)S(1)}, bf16[512,128]{1,0:T(8,128)(2,1)}, u32[]{:S(2)}) copy-start(bf16[512,128]{1,0:T(8,128)(2,1)} %refs_2_.1) | copy-start | bytes 393220
  63.4 35.4 %copy-start.2 = (bf16[512,128]{1,0:T(8,128)(2,1)S(1)}, bf16[512,128]{1,0:T(8,128)(2,1)}, u32[]{:S(2)}) copy-start(bf16[512,128]{1,0:T(8,128)(2,1)} %refs_3_.1) | copy-start | bytes 393220
  65.4 33.4 %all-to-all-start.3 = ((bf16[8,4,256,128]{3,2,1,0:T(8,128)(2,1)}), bf16[8,4,256,128]{3,2,1,0:T(8,128)(2,1)}, u32[]{:S(2)}, u32[]{:S(2)}) async-start(bf16[8,4,256,128]{3,2,1,0:T(8,128)(2,1)} %pick_blocks.5), calls=%async_computation.3 | async-start | bytes 4194304 | tf_op jit(solution)/shard_map/all_to_all | solution.py:179
where the time goes:
time: 144 us; the launch traced here: 143 us
  waiting for transfers between devices  47.9 us (33%)
  starting transfers between devices  40.7 us (28%)
  blocking collectives  33.6 us (23%)
  Pallas kernels  16.8 us (12%)
  local copies, waits for them, and re-layouts  2.31 us (2%)
  other arithmetic  1.83 us (1%)
    all_to_all x1, blocking collectives, attention(): lax.all_to_all(attended, 'kvh', split_axis=0, concat_axis=1, tiled=True)  33.6 us
    all_to_all x4, waiting for transfers between devices, to_row(): lax.all_to_all(array, 'ctx', split_axis=0, concat_axis=0, axis_index_grou...  31.7 us
    all_to_all x4, starting transfers between devices, to_row(): lax.all_to_all(array, 'ctx', split_axis=0, concat_axis=0, axis_index_grou...  21.3 us
    ppermute x3, waiting for transfers between devices, attention(): pairs.append(lax.ppermute(pairs[-1], 'ctx', SECOND if n % 2 else FIRST))  16.1 us
    ppermute x1, starting transfers between devices, attention(): other = lax.ppermute(shard, 'ctx', FIRST)  11.5 us
    pallas_call x1, Pallas kernels, attend(): pl.pallas_call(lambda *refs: attend_kernel(len(fetched), *refs), out_shap...  9.76 us
    ppermute x3, starting transfers between devices, attention(): pairs.append(lax.ppermute(pairs[-1], 'ctx', SECOND if n % 2 else FIRST))  7.92 us
    pallas_call x3, Pallas kernels, pick_blocks(): pl.pallas_call(lambda *refs: pick_kernel(slots, sources, *refs), out_shap...  5.48 us
  transfers between devices with their start and end apart: 8, of which 7 were waited for; matrix products, arithmetic and copies ran while one was open for 2% of the time, Pallas kernels for 3%

commit v1 on v0

--- a/solution.py
+++ b/solution.py
@@ -13,7 +13,7 @@
 PICKED_BLOCKS = 8
 SIZE_X, SIZE_Z, CORES = 4, 8, 2
 OFFSETS = (0, 1, -1, -2, 2, 3, -3, -4)
-BATCHES = ((0, 1), (2, 3), (4, 5, 6, 7))
+BATCHES = (((0, 1),), ((2, 3, 4, 5), (6, 7)))
 
 
 def pack_kernel(k_ref, v_ref, out_ref, sem):
@@ -39,13 +39,22 @@
     )(keys, values)
 
 
-def pick_kernel(slots, sources, wanted, *refs):
-    shards, out_ref = refs[:-1], refs[-1]
-
-    @pl.loop(0, out_ref.shape[0])
+def pick_kernel(slots, sources, first, wanted, *refs):
+    shards, (out_ref, buf, sem) = refs[: max(w for w, _ in sources) + 1], refs[-3:]
+
+    def send(d):
+        target = out_ref.at[d, pl.ds(first, len(slots))]
+        return pltpu.make_async_copy(buf.at[d], target, sem.at[d])
+
+    @pl.loop(0, buf.shape[0])
     def _(d):
-        for n, (slot, (which, first)) in enumerate(zip(slots, sources)):
-            out_ref[d, n] = shards[which][first + wanted[d, slot]]
+        for n, (slot, (which, begin)) in enumerate(zip(slots, sources)):
+            buf[d, n] = shards[which][begin + wanted[d, slot]]
+        send(d).start()
+
+    @pl.loop(0, buf.shape[0])
+    def _(d):
+        send(d).wait()
 
 
 GRANT = 16 * 2**20
@@ -53,21 +62,30 @@
 ATTEND_GRANT = 48 * 2**20
 
 
-def pick_blocks(wanted, slots, sources, shards):
+def pick_blocks(wanted, slots, sources, shards, first, total, partial):
     group = SIZE_X * CORES
-    shape = (group, len(slots), 2 * BLOCK_TOKENS, HEAD_SIZE)
+    block = (2 * BLOCK_TOKENS, HEAD_SIZE)
+    extra = [] if partial is None else [partial]
     return pl.pallas_call(
-        lambda *refs: pick_kernel(slots, sources, *refs),
-        out_shape=jax.ShapeDtypeStruct(shape, shards[0].dtype),
+        lambda *refs: pick_kernel(slots, sources, first, *refs),
+        out_shape=jax.ShapeDtypeStruct((group, total) + block, shards[0].dtype),
         grid_spec=pltpu.PrefetchScalarGridSpec(
             num_scalar_prefetch=1,
-            in_specs=[pl.BlockSpec(memory_space=pltpu.VMEM)] * len(shards),
-            out_specs=pl.BlockSpec(memory_space=pltpu.VMEM),
+            in_specs=[pl.BlockSpec(memory_space=pltpu.VMEM)] * len(shards)
+            + [pl.BlockSpec(memory_space=pl.ANY)] * len(extra),
+            out_specs=pl.BlockSpec(memory_space=pl.ANY),
+            scratch_shapes=[
+                pltpu.VMEM((group, len(slots)) + block, shards[0].dtype),
+                pltpu.SemaphoreType.DMA((group,)),
+            ],
         ),
+        input_output_aliases={1 + len(shards): 0} if extra else {},
         compiler_params=pltpu.CompilerParams(vmem_limit_bytes=GRANT),
-        cost_estimate=pl.CostEstimate(flops=0, bytes_accessed=4 * math.prod(shape), transcendentals=0),
+        cost_estimate=pl.CostEstimate(
+            flops=0, bytes_accessed=4 * group * len(slots) * math.prod(block), transcendentals=0
+        ),
         name="pick_blocks",
-    )(wanted, *shards)
+    )(wanted, *shards, *extra)
 
 
 def attend_kernel(batches, table, q_ref, k_ref, v_ref, *rest):
@@ -203,18 +221,16 @@
     for n in range(1, 4):
         pairs.append(lax.ppermute(pairs[-1], "ctx", SECOND if n % 2 else FIRST))
 
-    origin = {s: (pairs[s // 2], s % 2 * blocks) for s in range(SIZE_Z)}
     fetched = []
-    for slots in BATCHES:
-        arrays, sources = [], []
-        for s in slots:
-            array, first = origin[s]
-            which = next((i for i, a in enumerate(arrays) if a is array), None)
-            if which is None:
-                which = len(arrays)
-                arrays.append(array)
-            sources.append((which, first))
-        outgoing = pick_blocks(wanted, slots, sources, arrays)
+    for parts in BATCHES:
+        outgoing, first = None, 0
+        for slots in parts:
+            used = sorted({s // 2 for s in slots})
+            sources = [(used.index(s // 2), s % 2 * blocks) for s in slots]
+            outgoing = pick_blocks(
+                wanted, slots, sources, [pairs[u] for u in used], first, sum(map(len, parts)), outgoing
+            )
+            first += len(slots)
         fetched.append(to_row(outgoing))
     attended = attend(column, slot, queries, key_vector_rows, value_vector_rows, fetched)
     return lax.all_to_all(attended, "kvh", split_axis=0, concat_axis=1, tiled=True)

time: 144 us -> 151 us (1.049)
  starting transfers between devices: 40.7 us -> 30.7 us
  waiting for transfers between devices: 47.9 us -> 57.6 us
  blocking collectives: 33.6 us -> 42.6 us
    all_to_all x4 -> x2, starting transfers between devices: 21.3 us -> 9.46 us  [to_row(): lax.all_to_all(array, 'ctx', split_axis=0, concat_axis=0, axis_index_grou...]
    all_to_all x0 -> x1, blocking collectives: none -> 8.81 us  [to_row(): lax.all_to_all(array, 'ctx', split_axis=0, concat_axis=0, axis_index_grou...]
    all_to_all x4 -> x2, waiting for transfers between devices: 31.7 us -> 40.4 us  [to_row(): lax.all_to_all(array, 'ctx', split_axis=0, concat_axis=0, axis_index_grou...]
    ppermute x1, waiting for transfers between devices: 0.01 us -> 3.96 us  [attention(): other = lax.ppermute(shard, 'ctx', FIRST)]
    ppermute x3, waiting for transfers between devices: 16.1 us -> 13.2 us  [attention(): pairs.append(lax.ppermute(pairs[-1], 'ctx', SECOND if n % 2 else FIRST))]
    ppermute x3, starting transfers between devices: 7.92 us -> 9.75 us  [attention(): pairs.append(lax.ppermute(pairs[-1], 'ctx', SECOND if n % 2 else FIRST))]
  transfers between devices with their start and end apart: 8 -> 6, of which waited for: 7 -> 5; matrix products, arithmetic and copies ran while one was open for 2% -> 1% of each run, Pallas kernels for 3% -> 4%
where the time goes in v1:
time: 151 us; the launch traced here: 150 us
  waiting for transfers between devices  57.6 us (38%)
  blocking collectives  42.6 us (28%)
  starting transfers between devices  30.7 us (20%)
  Pallas kernels  15.9 us (11%)
  other arithmetic  1.83 us (1%)
  local copies, waits for them, and re-layouts  1.64 us (1%)
    all_to_all x2, waiting for transfers between devices, to_row(): lax.all_to_all(array, 'ctx', split_axis=0, concat_axis=0, axis_index_grou...  40.4 us
    all_to_all x1, blocking collectives, attention(): lax.all_to_all(attended, 'kvh', split_axis=0, concat_axis=1, tiled=True)  33.8 us
    ppermute x3, waiting for transfers between devices, attention(): pairs.append(lax.ppermute(pairs[-1], 'ctx', SECOND if n % 2 else FIRST))  13.2 us
    ppermute x1, starting transfers between devices, attention(): other = lax.ppermute(shard, 'ctx', FIRST)  11.5 us
    ppermute x3, starting transfers between devices, attention(): pairs.append(lax.ppermute(pairs[-1], 'ctx', SECOND if n % 2 else FIRST))  9.75 us
    all_to_all x2, starting transfers between devices, to_row(): lax.all_to_all(array, 'ctx', split_axis=0, concat_axis=0, axis_index_grou...  9.46 us
    pallas_call x1, Pallas kernels, attend(): pl.pallas_call(lambda *refs: attend_kernel(len(fetched), *refs), out_shap...  8.99 us
    all_to_all x1, blocking collectives, to_row(): lax.all_to_all(array, 'ctx', split_axis=0, concat_axis=0, axis_index_grou...  8.81 us
  transfers between devices with their start and end apart: 6, of which 5 were waited for; matrix products, arithmetic and copies ran while one was open for 1% of the time, Pallas kernels for 4%

profile of v1, /device:TPU:1, one launch (start us, length us, event | category | flops | bytes accessed | tf_op | source)
XLA Modules:
  0.0 150.4 jit_solution(10610207607427281546)
XLA Ops:
  0.0 1.6 %pack.1 = bf16[4,256,128]{2,1,0:T(8,128)(2,1)} custom-call(bf16[512,128]{1,0:T(8,128)(2,1)} %refs_2_.1, bf16[512,128]{1,0:T(8,128)(2,1)} %refs_3_.1), custom_call_target="tpu_custom_call" | custom-call | bytes 524288 | tf_op jit(solution)/shard_map/pack/pallas_call | solution.py:30
  1.6 11.5 %collective-permute-start = (bf16[4,256,128]{2,1,0:T(8,128)(2,1)}, bf16[4,256,128]{2,1,0:T(8,128)(2,1)S(1)}, u32[]{:S(2)}, u32[]{:S(2)}) collective-permute-start(bf16[4,256,128]{2,1,0:T(8,128)(2,1)} %pack.1), channel_id=1, source_target_pairs={{0,16},{8,120},{16,0},{24,40},{32,48},{40,24},{48,32},{56,72},{64,... | collective-permute-start | bytes 786440 | tf_op jit(solution)/shard_map/ppermute | solution.py:219
  13.1 4.0 %collective-permute-done = bf16[4,256,128]{2,1,0:T(8,128)(2,1)S(1)} collective-permute-done((bf16[4,256,128]{2,1,0:T(8,128)(2,1)}, bf16[4,256,128]{2,1,0:T(8,128)(2,1)S(1)}, u32[]{:S(2)}, u32[]{:S(2)}) %collective-permute-start) | collective-permute-done | bytes 262176 | tf_op jit(solution)/shard_map/ppermute | solution.py:219
  17.0 1.0 pad_maximum_fusion.refs_1_
  18.0 1.9 %collective-permute-start.1 = (bf16[8,256,128]{2,1,0:T(8,128)(2,1)S(1)}, bf16[8,256,128]{2,1,0:T(8,128)(2,1)S(1)}, u32[]{:S(2)}, u32[]{:S(2)}) collective-permute-start(bf16[8,256,128]{2,1,0:T(8,128)(2,1)S(1)} %pad_maximum_fusion.refs_1_), channel_id=1, source_target_pairs={{0,112},{8,24},{16,32},{24,8},{32,16},{40,56},{48,64},{56,40},{64,... | collective-permute-start | bytes 1572872 | tf_op jit(solution)/shard_map/ppermute | solution.py:222
  20.0 8.3 %collective-permute-done.1.refs_1_ = bf16[8,256,128]{2,1,0:T(8,128)(2,1)S(1)} collective-permute-done((bf16[8,256,128]{2,1,0:T(8,128)(2,1)S(1)}, bf16[8,256,128]{2,1,0:T(8,128)(2,1)S(1)}, u32[]{:S(2)}, u32[]{:S(2)}) %collective-permute-start.1) | collective-permute-done | bytes 524320 | tf_op jit(solution)/shard_map/ppermute | solution.py:222
  28.3 4.6 %collective-permute-start.2 = (bf16[8,256,128]{2,1,0:T(8,128)(2,1)S(1)}, bf16[8,256,128]{2,1,0:T(8,128)(2,1)S(1)}, u32[]{:S(2)}, u32[]{:S(2)}) collective-permute-start(bf16[8,256,128]{2,1,0:T(8,128)(2,1)S(1)} %collective-permute-done.1.refs_1_), channel_id=1, source_target_pairs={{0,16},{8,120},{16,0},{24,40},{32,48},{40,24},{48,32},{56,72},{64,... | collective-permute-start | bytes 1572872 | tf_op jit(solution)/shard_map/ppermute | solution.py:222
  32.8 0.7 multiply_add_fusion
  33.5 0.1 slice.7
  33.6 0.1 broadcast_in_dim.30
  33.7 0.1 slice.6
  33.8 0.1 eq.64
  33.9 0.1 select_reduce_fusion
  34.0 0.1 all_to_all.27
  34.0 8.8 %all_to_all.40 = s32[8,1,8]{2,1,0:T(1,128)S(1)} all-to-all(s32[8,1,8]{2,1,0:T(1,128)S(1)} %bitcast.14), channel_id=1, replica_groups={{0,8,128,136,256,264,384,392},{16,24,144,152,272,280,400,408},{32,40,16..., dimensions={0} | all-to-all | bytes 512 | tf_op jit(solution)/shard_map/all_to_all | solution.py:197
  42.9 1.6 %pick_blocks.3 = bf16[8,2,256,128]{3,2,1,0:T(8,128)(2,1)} custom-call(s32[8,8]{1,0:T(8,128)S(1)} %bitcast.10, bf16[8,256,128]{2,1,0:T(8,128)(2,1)S(1)} %pad_maximum_fusion.refs_1_), custom_call_target="tpu_custom_call" | custom-call | bytes 2097152 | tf_op jit(solution)/shard_map/pick_blocks/pallas_call | solution.py:69
  44.5 4.2 %all-to-all-start.1 = ((bf16[8,2,256,128]{3,2,1,0:T(8,128)(2,1)}), bf16[8,2,256,128]{3,2,1,0:T(8,128)(2,1)S(1)}, u32[]{:S(2)}, u32[]{:S(2)}) async-start(bf16[8,2,256,128]{3,2,1,0:T(8,128)(2,1)} %pick_blocks.3), calls=%async_computation.1 | async-start | bytes 2097152 | tf_op jit(solution)/shard_map/all_to_all | solution.py:197
  48.7 3.3 %collective-permute-start.3 = (bf16[8,256,128]{2,1,0:T(8,128)(2,1)S(1)}, bf16[8,256,128]{2,1,0:T(8,128)(2,1)S(1)}, u32[]{:S(2)}, u32[]{:S(2)}) collective-permute-start(bf16[8,256,128]{2,1,0:T(8,128)(2,1)S(1)} %collective-permute-done.2.refs_2_), channel_id=1, source_target_pairs={{0,112},{8,24},{16,32},{24,8},{32,16},{40,56},{48,64},{56,40},{64,... | collective-permute-start | bytes 1572872 | tf_op jit(solution)/shard_map/ppermute | solution.py:222
  51.9 2.0 %pick_blocks.4.refs_2_ = bf16[8,6,256,128]{3,2,1,0:T(8,128)(2,1)} custom-call(s32[8,8]{1,0:T(8,128)S(1)} %bitcast.11, bf16[8,256,128]{2,1,0:T(8,128)(2,1)S(1)} %collective-permute-done.1.refs_1_, bf16[8,256,128]{2,1,0:T(8,128)(2,1)S(1)} %collective-permute-done.2.refs_2_), custom_call_target="tpu_custom_call" | custom-call | bytes 4194304 | tf_op jit(solution)/shard_map/pick_blocks/pallas_call | solution.py:69
  53.9 4.9 %collective-permute-done.3.refs_1_ = bf16[8,256,128]{2,1,0:T(8,128)(2,1)S(1)} collective-permute-done((bf16[8,256,128]{2,1,0:T(8,128)(2,1)S(1)}, bf16[8,256,128]{2,1,0:T(8,128)(2,1)S(1)}, u32[]{:S(2)}, u32[]{:S(2)}) %collective-permute-start.3) | collective-permute-done | bytes 524320 | tf_op jit(solution)/shard_map/ppermute | solution.py:222
  58.9 1.7 %pick_blocks.5 = bf16[8,6,256,128]{3,2,1,0:T(8,128)(2,1)} custom-call(s32[8,8]{1,0:T(8,128)S(1)} %bitcast.12, bf16[8,256,128]{2,1,0:T(8,128)(2,1)S(1)} %collective-permute-done.3.refs_1_, bf16[8,6,256,128]{3,2,1,0:T(8,128)(2,1)} %pick_blocks.4.refs_2_), custom_call_target="tpu_custom_call", output_to_operand_aliasing={{}: (2, {})} | custom-call | bytes 2097152 | tf_op jit(solution)/shard_map/pick_blocks/pallas_call | solution.py:69
  60.6 0.0 copy-start
  60.6 0.0 copy-start.1
  60.6 0.0 copy-start.2
  60.6 3.0 %all-to-all-done.1 = bf16[8,2,256,128]{3,2,1,0:T(8,128)(2,1)S(1)} async-done(((bf16[8,2,256,128]{3,2,1,0:T(8,128)(2,1)}), bf16[8,2,256,128]{3,2,1,0:T(8,128)(2,1)S(1)}, u32[]{:S(2)}, u32[]{:S(2)}) %all-to-all-start.1) | async-done | bytes 1048608 | tf_op jit(solution)/shard_map/all_to_all | solution.py:197
  63.7 5.3 %all-to-all-start.2 = ((bf16[8,6,256,128]{3,2,1,0:T(8,128)(2,1)}), bf16[8,6,256,128]{3,2,1,0:T(8,128)(2,1)}, u32[]{:S(2)}, u32[]{:S(2)}) async-start(bf16[8,6,256,128]{3,2,1,0:T(8,128)(2,1)} %pick_blocks.5), calls=%async_computation.2 | async-start | bytes 6291456 | tf_op jit(solution)/shard_map/all_to_all | solution.py:197
  69.0 0.1 stack_reshape.6
  69.0 0.1 stack_reshape.7
  69.1 37.4 %all-to-all-done.2 = bf16[8,6,256,128]{3,2,1,0:T(8,128)(2,1)} async-done(((bf16[8,6,256,128]{3,2,1,0:T(8,128)(2,1)}), bf16[8,6,256,128]{3,2,1,0:T(8,128)(2,1)}, u32[]{:S(2)}, u32[]{:S(2)}) %all-to-all-start.2) | async-done | bytes 3145760 | tf_op jit(solution)/shard_map/all_to_all | solution.py:197
  106.5 9.0 %attend.1 = bf16[512,1024]{1,0:T(8,128)(2,1)S(1)} custom-call(s32[2,32]{1,0:T(2,128)S(1)} %pad_add_fusion.refs_0_, bf16[512,1024]{1,0:T(8,128)(2,1)S(1)} %copy-done, bf16[512,128]{1,0:T(8,128)(2,1)S(1)} %copy-done.1, bf16[512,128]{1,0:T(8,128)(2,1)S(1)} %copy-done.2, bf16[16,256,128]{2,1,0:T(8,128)(2,1)S(1)} %bitcast.8, bf16[48,256,128]{2,1,0:T(8,128)(2,1)} %bitcast.3.refs_5_), custom_call_target="tpu_custom_call" | custom-call | tf_op jit(solution)/shard_map/attend/pallas_call | solution.py:167
  115.5 33.8 %all_to_all.41 = bf16[8,64,1024]{2,1,0:T(8,128)(2,1)S(1)} all-to-all(bf16[8,64,1024]{2,1,0:T(8,128)(2,1)S(1)} %bitcast.9), channel_id=1, replica_groups=mesh['ctx'=64,'kvh'=8] {'kvh'}, dimensions={0} | all-to-all | bytes 2097152 | tf_op jit(solution)/shard_map/all_to_all | solution.py:236
  149.3 1.1 copy.11
  (6 shorter events, 0.0 us)
Async XLA Ops:
  1.6 15.4 %collective-permute-start = (bf16[4,256,128]{2,1,0:T(8,128)(2,1)}, bf16[4,256,128]{2,1,0:T(8,128)(2,1)S(1)}, u32[]{:S(2)}, u32[]{:S(2)}) collective-permute-start(bf16[4,256,128]{2,1,0:T(8,128)(2,1)} %pack.1), channel_id=1, source_target_pairs={{0,16},{8,120},{16,0},{24,40},{32,48},{40,24},{48,32},{56,72},{64,... | collective-permute-start | bytes 786440 | tf_op jit(solution)/shard_map/ppermute | solution.py:219
  18.0 10.2 %collective-permute-start.1 = (bf16[8,256,128]{2,1,0:T(8,128)(2,1)S(1)}, bf16[8,256,128]{2,1,0:T(8,128)(2,1)S(1)}, u32[]{:S(2)}, u32[]{:S(2)}) collective-permute-start(bf16[8,256,128]{2,1,0:T(8,128)(2,1)S(1)} %pad_maximum_fusion.refs_1_), channel_id=1, source_target_pairs={{0,112},{8,24},{16,32},{24,8},{32,16},{40,56},{48,64},{56,40},{64,... | collective-permute-start | bytes 1572872 | tf_op jit(solution)/shard_map/ppermute | solution.py:222
  28.3 20.4 %collective-permute-start.2 = (bf16[8,256,128]{2,1,0:T(8,128)(2,1)S(1)}, bf16[8,256,128]{2,1,0:T(8,128)(2,1)S(1)}, u32[]{:S(2)}, u32[]{:S(2)}) collective-permute-start(bf16[8,256,128]{2,1,0:T(8,128)(2,1)S(1)} %collective-permute-done.1.refs_1_), channel_id=1, source_target_pairs={{0,16},{8,120},{16,0},{24,40},{32,48},{40,24},{48,32},{56,72},{64,... | collective-permute-start | bytes 1572872 | tf_op jit(solution)/shard_map/ppermute | solution.py:222
  44.5 19.2 %all-to-all-start.1 = ((bf16[8,2,256,128]{3,2,1,0:T(8,128)(2,1)}), bf16[8,2,256,128]{3,2,1,0:T(8,128)(2,1)S(1)}, u32[]{:S(2)}, u32[]{:S(2)}) async-start(bf16[8,2,256,128]{3,2,1,0:T(8,128)(2,1)} %pick_blocks.3), calls=%async_computation.1 | async-start | bytes 2097152 | tf_op jit(solution)/shard_map/all_to_all | solution.py:197
  48.7 10.2 %collective-permute-start.3 = (bf16[8,256,128]{2,1,0:T(8,128)(2,1)S(1)}, bf16[8,256,128]{2,1,0:T(8,128)(2,1)S(1)}, u32[]{:S(2)}, u32[]{:S(2)}) collective-permute-start(bf16[8,256,128]{2,1,0:T(8,128)(2,1)S(1)} %collective-permute-done.2.refs_2_), channel_id=1, source_target_pairs={{0,112},{8,24},{16,32},{24,8},{32,16},{40,56},{48,64},{56,40},{64,... | collective-permute-start | bytes 1572872 | tf_op jit(solution)/shard_map/ppermute | solution.py:222
  60.6 45.9 %copy-start = (bf16[512,1024]{1,0:T(8,128)(2,1)S(1)}, bf16[512,1024]{1,0:T(8,128)(2,1)}, u32[]{:S(2)}) copy-start(bf16[512,1024]{1,0:T(8,128)(2,1)} %refs_1_.1) | copy-start | bytes 3145732
  60.6 45.9 %copy-start.1 = (bf16[512,128]{1,0:T(8,128)(2,1)S(1)}, bf16[512,128]{1,0:T(8,128)(2,1)}, u32[]{:S(2)}) copy-start(bf16[512,128]{1,0:T(8,128)(2,1)} %refs_2_.1) | copy-start | bytes 393220
  60.6 45.9 %copy-start.2 = (bf16[512,128]{1,0:T(8,128)(2,1)S(1)}, bf16[512,128]{1,0:T(8,128)(2,1)}, u32[]{:S(2)}) copy-start(bf16[512,128]{1,0:T(8,128)(2,1)} %refs_3_.1) | copy-start | bytes 393220
  63.7 42.9 %all-to-all-start.2 = ((bf16[8,6,256,128]{3,2,1,0:T(8,128)(2,1)}), bf16[8,6,256,128]{3,2,1,0:T(8,128)(2,1)}, u32[]{:S(2)}, u32[]{:S(2)}) async-start(bf16[8,6,256,128]{3,2,1,0:T(8,128)(2,1)} %pick_blocks.5), calls=%async_computation.2 | async-start | bytes 6291456 | tf_op jit(solution)/shard_map/all_to_all | solution.py:197
